TPU v7x, 32 devices: a whole 2x2x4 slice. The times are simulated.
32 devices in a mesh: dp: 8 (over z, core), tensor: 4 (over y, x).
Axes of the slice: x: 2, y: 2, z: 4, core: 2. Of those that a mesh axis runs over, the one named last changes fastest.
Arguments:
- hidden_acts: bfloat16 [16384, 14336], P('dp', 'tensor'), may hold values from -6 to 6
- out_grads: bfloat16 [16384, 4096], P('dp', 'tensor'), may hold values from -6 to 6
- proj_in: bfloat16 [14336, 64], P('tensor'), may hold values from -0.046875 to 0.046875
- proj_out: bfloat16 [4096, 64], P('tensor'), may hold values from -0.09375 to 0.09375
- segments: int32 [32, 16384], P(None, 'dp'), may hold values from 0 to 1, as said below
- doc_counts: int32 [8], P('dp'), may hold values from 10 to 32
Outputs:
- doc_grads: bfloat16 [256, 4096], P('dp', 'tensor')
- fisher: float32 [4096, 4096], P('dp', 'tensor')
Inputs may be any that keep to these rules, and one draw needn't show every extreme that they name: `segments`: every token belongs to exactly one slot of its shard; within one shard's 2048 tokens the slots 0 to 31 are contiguous runs in that order, each holding at least one token.
All inputs are finite; a program needn't handle non-finite values.
Results may differ from a plain program's by a relative error of at most 0.0062.
Values may be sent and summed in bfloat16 or wider, within the bound.
No kernel may reach another device: no remote copies, remote signals or barrier semaphores. Data moves between devices by JAX's collectives and lax.ppermute only.
A program may use at most 64 MiB of HBM per device.

v0:
```python
import jax
import jax.numpy as jnp
from jax import lax
from jax.sharding import PartitionSpec as P

RANK = 64


def doc_sums_of(seg_live, dy_proj, x_proj):
    row_count = x_proj.shape[0]
    block_rows = 512
    summed = jnp.zeros((seg_live.shape[0], RANK * RANK), jnp.float32)
    for offset in range(0, row_count, block_rows):
        outer = (
            (
                dy_proj[offset : offset + block_rows, :, None]
                * x_proj[offset : offset + block_rows, None, :]
            )
            .reshape(block_rows, RANK * RANK)
            .astype(jnp.bfloat16)
        )
        summed = summed + jnp.dot(
            seg_live[:, offset : offset + block_rows], outer, preferred_element_type=jnp.float32
        )
    return summed


def transpose_product(left, right):
    return lax.dot_general(
        left, right, (((0,), (0,)), ((), ())), preferred_element_type=jnp.float32
    )


def per_device(hidden_acts, out_grads, proj_in, proj_out, segments, doc_counts):
    x_part = jnp.dot(hidden_acts, proj_in, preferred_element_type=jnp.float32)
    dy_part = jnp.dot(out_grads, proj_out, preferred_element_type=jnp.float32)
    partial_proj = jnp.concatenate([dy_part, x_part], axis=1)
    doc_total = segments.shape[0]
    live_docs = (jnp.arange(doc_total, dtype=jnp.int32) < doc_counts[0]).astype(jnp.int32)
    seg_int = segments * live_docs[:, None]
    seg_live = seg_int.astype(jnp.bfloat16)
    local_tokens = jnp.sum(seg_int).astype(jnp.float32)
    stacked = lax.psum(partial_proj, "tensor")
    doc_sums = doc_sums_of(seg_live, stacked[:, :RANK], stacked[:, RANK:])
    doc_grads = doc_sums.astype(jnp.bfloat16)
    col_width = doc_grads.shape[1] // lax.axis_size("tensor")
    col_block = lax.dynamic_slice_in_dim(
        doc_grads, lax.axis_index("tensor") * col_width, col_width, 1
    )
    total_tokens = lax.psum(local_tokens, "dp")
    dp_size = lax.axis_size("dp")
    row_width = doc_grads.shape[1] // dp_size
    split_rows = doc_grads.reshape(doc_total, dp_size, row_width)
    gathered_rows = lax.all_to_all(
        split_rows, "dp", split_axis=1, concat_axis=0, tiled=True
    ).reshape(doc_total * dp_size, row_width)
    fisher_block = transpose_product(
        gathered_rows, lax.all_gather(col_block, "dp", axis=0, tiled=True)
    )
    return (col_block, fisher_block / total_tokens)


def solution(mesh):
    return jax.shard_map(
        per_device,
        mesh=mesh,
        in_specs=(
            P("dp", "tensor"),
            P("dp", "tensor"),
            P("tensor", None),
            P("tensor", None),
            P(None, "dp"),
            P("dp"),
        ),
        out_specs=(P("dp", "tensor"), P("dp", "tensor")),
        check_vma=False,
    )
```

profile of v0, /device:TPU:0, one launch (start us, length us, event | category | flops | bytes accessed | tf_op | source)
XLA Modules:
  0.0 138.1 jit_solution(17943158903537048808)
XLA Ops:
  7.2 0.0 copy-start
  7.2 0.0 all-reduce.2.cloned.1.call-start
  7.2 3.6 %fusion.7 = f32[2048,64]{0,1:T(8,128)S(1)} fusion(bf16[2048,1024]{1,0:T(8,128)(2,1)} %param.7, bf16[1024,64]{0,1:T(8,128)(2,1)} %param.9), kind=kOutput, calls=%fused_computation.21 | convolution fusion | flops 268435456 | bytes 4849664 | tf_op jit(solution)/shard_map/dot_general | solution.py:36
  10.9 0.0 copy-done
  10.9 0.0 copy-start.2
  10.9 9.7 %fusion.8 = f32[2048,64]{0,1:T(8,128)S(1)} fusion(bf16[2048,3584]{1,0:T(8,128)(2,1)} %param.6, bf16[3584,64]{0,1:T(8,128)(2,1)S(1)} %copy-done), kind=kOutput, calls=%fused_computation.22 | convolution fusion | flops 939524096 | bytes 15663104 | tf_op jit(solution)/shard_map/dot_general | solution.py:35
  20.6 1.0 pad_maximum_fusion
  21.6 0.0 all-reduce.2.cloned.1.call-update
  22.3 0.0 copy-done.2
  22.3 0.8 multiply_reduce_fusion
  23.1 53.9 %all-reduce.2.cloned.1.call-done = f32[2048,128]{0,1:T(8,128)} async-done(((f32[2048,128]{0,1:T(8,128)}), f32[2048,128]{0,1:T(8,128)}) %all-reduce.2.cloned.1.call-update) | async-done | bytes 1048592 | tf_op jit(solution)/shard_map/psum | solution.py:43
  77.0 1.4 fusion.6
  78.3 3.3 %multiply_convert_fusion.2 = (bf16[512,64,64]{0,2,1:T(8,128)(2,1)S(1)}, bf16[512,64,64]{0,2,1:T(8,128)(2,1)S(1)}) fusion(f32[512,64]{0,1:T(8,128)S(1)} %get-tuple-element.6, f32[512,64]{0,1:T(8,128)S(1)} %get-tuple-element.7, f32[512,64]{0,1:T(8,128)S(1)} %get-tuple-element.8, f32[512,64]{0,1:T(8,128)S(1)} %get-tuple-element.9), kind=kLoop, calls=%fused_computation.2 | loop fusion | flops 8388608 | bytes 8912896 | tf_op jit(solution)/shard_map/convert_element_type | solution.py:20
  81.6 1.3 fusion.4
  82.9 1.3 convolution_add_fusion.2
  84.2 3.3 %multiply_convert_fusion = (bf16[512,64,64]{0,2,1:T(8,128)(2,1)S(1)}, bf16[512,64,64]{0,2,1:T(8,128)(2,1)S(1)}) fusion(f32[512,64]{0,1:T(8,128)S(1)} %get-tuple-element.3, f32[512,64]{0,1:T(8,128)S(1)} %get-tuple-element.2, f32[512,64]{0,1:T(8,128)S(1)} %get-tuple-element.4, f32[512,64]{0,1:T(8,128)S(1)} %get-tuple-element.5), kind=kLoop, calls=%fused_computation | loop fusion | flops 8388608 | bytes 8912896 | tf_op jit(solution)/shard_map/convert_element_type | solution.py:20
  87.5 1.3 convolution_add_fusion.1
  88.8 1.3 fusion
  90.2 0.7 copy.19
  90.9 4.6 %all-to-all-start = ((bf16[32,8,512]{2,0,1:T(8,128)(2,1)}), bf16[32,8,512]{2,0,1:T(8,128)(2,1)S(1)}, u32[]{:S(2)}, u32[]{:S(2)}) async-start(bf16[32,8,512]{2,0,1:T(8,128)(2,1)} %bitcast.23), calls=%async_computation | async-start | bytes 524288 | tf_op jit(solution)/shard_map/all_to_all | solution.py:54
  96.2 17.8 %psum.15 = f32[]{:T(128)} all-reduce(f32[]{:T(128)S(6)} %convert_element_type.51), channel_id=1, replica_groups=mesh['dp'=8,'tensor'=4] {'dp'}, use_global_device_ids=true, to_apply=%region_2.0 | all-reduce | flops 1 | bytes 8 | tf_op jit(solution)/shard_map/psum | solution.py:50
  113.9 0.0 copy-start.1
  113.9 14.9 %all_gather.3 = bf16[256,1024]{1,0:T(8,128)(2,1)S(1)} all-gather(bf16[32,1024]{1,0:T(8,128)(2,1)S(1)} %constant_dynamic-slice_fusion), channel_id=1, replica_groups=mesh['dp'=8,'tensor'=4] {'dp'}, dimensions={0}, use_global_device_ids=true | all-gather | bytes 589824 | tf_op jit(solution)/shard_map/all_gather | solution.py:58
  128.9 0.0 all-to-all-done
  128.9 2.4 %convolution_divide_fusion = f32[512,1024]{1,0:T(8,128)} fusion(bf16[256,512]{1,0:T(8,128)(2,1)S(1)} %bitcast.30, bf16[256,1024]{1,0:T(8,128)(2,1)S(1)} %all_gather.3, f32[]{:T(128)} %psum.15), kind=kOutput, calls=%fused_computation.8 | convolution fusion | flops 268959744 | bytes 2883588 | tf_op jit(solution)/shard_map/dot_general | solution.py:29
  131.3 0.0 copy-done.1
  (2 shorter events, 0.0 us)
Async XLA Ops:
  7.2 3.7 %copy-start = (bf16[3584,64]{0,1:T(8,128)(2,1)S(1)}, bf16[3584,64]{0,1:T(8,128)(2,1)}, u32[]{:S(2)}) copy-start(bf16[3584,64]{0,1:T(8,128)(2,1)} %param.8) | copy-start | bytes 1376260
  7.2 69.8 %all-reduce.2.cloned.1.call-start = ((), (), s32[]{:S(2)}) async-start(), calls=%async_computation.1 | async-start | bytes 2097152 | tf_op jit(solution)/shard_map/psum | solution.py:43
  10.9 11.5 %copy-start.2 = (s32[32,2048]{1,0:T(8,128)S(1)}, s32[32,2048]{1,0:T(8,128)}, u32[]{:S(2)}) copy-start(s32[32,2048]{1,0:T(8,128)} %param.10) | copy-start | bytes 786436
  90.9 38.0 %all-to-all-start = ((bf16[32,8,512]{2,0,1:T(8,128)(2,1)}), bf16[32,8,512]{2,0,1:T(8,128)(2,1)S(1)}, u32[]{:S(2)}, u32[]{:S(2)}) async-start(bf16[32,8,512]{2,0,1:T(8,128)(2,1)} %bitcast.23), calls=%async_computation | async-start | bytes 524288 | tf_op jit(solution)/shard_map/all_to_all | solution.py:54
  113.9 17.3 %copy-start.1 = (bf16[32,1024]{1,0:T(8,128)(2,1)}, bf16[32,1024]{1,0:T(8,128)(2,1)S(1)}, u32[]{:S(2)}) copy-start(bf16[32,1024]{1,0:T(8,128)(2,1)S(1)} %constant_dynamic-slice_fusion) | copy-start | bytes 196612
Sparse Core Ops, SparseCore 0:
  21.8 55.1 all-reduce.1
where the time goes:
time: 138 us
  waiting for transfers between devices  53.9 us (39%)
  blocking collectives  32.7 us (24%)
  matrix products  21 us (15%)
  between operations  15.4 us (11%)
  other arithmetic  8.34 us (6%)
  starting transfers between devices  4.65 us (3%)
  local copies, waits for them, and re-layouts  2.11 us (2%)
    psum x1, waiting for transfers between devices, per_device(): stacked = lax.psum(partial_proj, 'tensor')  53.9 us
    psum x1, blocking collectives, per_device(): total_tokens = lax.psum(local_tokens, 'dp')  17.8 us
    all_gather x1, blocking collectives, per_device(): lax.all_gather(col_block, 'dp', axis=0, tiled=True)  14.9 us
    dot_general x1, matrix products, per_device(): x_part = jnp.dot(hidden_acts, proj_in, preferred_element_type=jnp.float32)  9.71 us
    convert_element_type x2, other arithmetic, doc_sums_of(): outer = (dy_proj[offset:offset + block_rows, :, None] * x_proj[offset:off...  6.53 us
    dot_general x4, matrix products, doc_sums_of(): jnp.dot(seg_live[:, offset:offset + block_rows], outer, preferred_element...  5.29 us
    all_to_all x1, starting transfers between devices, per_device(): lax.all_to_all(split_rows, 'dp', split_axis=1, concat_axis=0, tiled=True)  4.61 us
    dot_general x1, matrix products, per_device(): dy_part = jnp.dot(out_grads, proj_out, preferred_element_type=jnp.float32)  3.63 us
  transfers between devices with their start and end apart: 2, of which 1 were waited for; matrix products, arithmetic and copies ran while one was open for 1% of the time, Pallas kernels for 0%

commit v1 on v0

--- a/solution.py
+++ b/solution.py
@@ -40,7 +40,7 @@
     seg_int = segments * live_docs[:, None]
     seg_live = seg_int.astype(jnp.bfloat16)
     local_tokens = jnp.sum(seg_int).astype(jnp.float32)
-    stacked = lax.psum(partial_proj, "tensor")
+    stacked = jnp.sum(lax.all_gather(partial_proj, "tensor"), axis=0)
     doc_sums = doc_sums_of(seg_live, stacked[:, :RANK], stacked[:, RANK:])
     doc_grads = doc_sums.astype(jnp.bfloat16)
     col_width = doc_grads.shape[1] // lax.axis_size("tensor")

time: 138 us -> 148 us (1.072)
  other arithmetic: 8.34 us -> 13.2 us
  local copies, waits for them, and re-layouts: 2.11 us -> 6.88 us
    all_gather x0 -> x1, waiting for transfers between devices: none -> 54 us  [per_device(): stacked = jnp.sum(lax.all_gather(partial_proj, 'tensor'), axis=0)]
    psum x1 -> x0, waiting for transfers between devices: 53.9 us -> none  [per_device(): stacked = lax.psum(partial_proj, 'tensor')]
    all_gather x0 -> x1, local copies, waits for them, and re-layouts: none -> 6.04 us  [per_device(): stacked = jnp.sum(lax.all_gather(partial_proj, 'tensor'), axis=0)]
    reduce_sum x0 -> x1, other arithmetic: none -> 4.84 us  [per_device(): stacked = jnp.sum(lax.all_gather(partial_proj, 'tensor'), axis=0)]
where the time goes in v1:
time: 148 us
  waiting for transfers between devices  54 us (36%)
  blocking collectives  32.7 us (22%)
  matrix products  21 us (14%)
  between operations  15.4 us (10%)
  other arithmetic  13.2 us (9%)
  local copies, waits for them, and re-layouts  6.88 us (5%)
  starting transfers between devices  4.65 us (3%)
    all_gather x1, waiting for transfers between devices, per_device(): stacked = jnp.sum(lax.all_gather(partial_proj, 'tensor'), axis=0)  54 us
    psum x1, blocking collectives, per_device(): total_tokens = lax.psum(local_tokens, 'dp')  17.8 us
    all_gather x1, blocking collectives, per_device(): lax.all_gather(col_block, 'dp', axis=0, tiled=True)  14.9 us
    dot_general x1, matrix products, per_device(): x_part = jnp.dot(hidden_acts, proj_in, preferred_element_type=jnp.float32)  9.71 us
    convert_element_type x2, other arithmetic, doc_sums_of(): outer = (dy_proj[offset:offset + block_rows, :, None] * x_proj[offset:off...  6.53 us
    all_gather x1, local copies, waits for them, and re-layouts, per_device(): stacked = jnp.sum(lax.all_gather(partial_proj, 'tensor'), axis=0)  6.04 us
    dot_general x4, matrix products, doc_sums_of(): jnp.dot(seg_live[:, offset:offset + block_rows], outer, preferred_element...  5.29 us
    reduce_sum x1, other arithmetic, per_device(): stacked = jnp.sum(lax.all_gather(partial_proj, 'tensor'), axis=0)  4.84 us
  transfers between devices with their start and end apart: 2, of which 1 were waited for; matrix products, arithmetic and copies ran while one was open for 1% of the time, Pallas kernels for 0%

profile of v1, /device:TPU:0, one launch (start us, length us, event | category | flops | bytes accessed | tf_op | source)
XLA Modules:
  0.0 147.9 jit_solution(15985096232101240502)
XLA Ops:
  7.2 0.0 copy-start
  7.2 0.0 all-gather.3.cloned.1.call-start
  7.2 3.6 %fusion.7 = f32[2048,64]{0,1:T(8,128)S(1)} fusion(bf16[2048,1024]{1,0:T(8,128)(2,1)} %param.7, bf16[1024,64]{0,1:T(8,128)(2,1)} %param.9), kind=kOutput, calls=%fused_computation.21 | convolution fusion | flops 268435456 | bytes 4849664 | tf_op jit(solution)/shard_map/dot_general | solution.py:36
  10.9 0.0 copy-done
  10.9 0.0 copy-start.2
  10.9 9.7 %fusion.8 = f32[2048,64]{0,1:T(8,128)S(1)} fusion(bf16[2048,3584]{1,0:T(8,128)(2,1)} %param.6, bf16[3584,64]{0,1:T(8,128)(2,1)S(1)} %copy-done), kind=kOutput, calls=%fused_computation.22 | convolution fusion | flops 939524096 | bytes 15663104 | tf_op jit(solution)/shard_map/dot_general | solution.py:35
  20.6 1.1 pad_maximum_fusion
  21.6 0.0 all-gather.3.cloned.1.call-update
  22.3 0.0 copy-done.2
  22.3 0.8 multiply_reduce_fusion
  23.1 54.0 %all-gather.3.cloned.1.call-done = f32[8192,128]{0,1:T(8,128)} async-done(((f32[2048,128]{0,1:T(8,128)}), f32[8192,128]{0,1:T(8,128)}) %all-gather.3.cloned.1.call-update) | async-done | bytes 4194320 | tf_op jit(solution)/shard_map/all_gather | solution.py:43
  77.1 6.0 %reshape.46 = f32[4,2048,128]{1,0,2:T(4,128)} reshape(f32[8192,128]{0,1:T(8,128)} %all-gather.3.cloned.1.call-done) | data formatting | bytes 8388608 | tf_op jit(solution)/shard_map/all_gather | solution.py:43
  83.2 4.8 %reduce_sum.18 = f32[2048,128]{0,1:T(8,128)S(1)} reduce(f32[4,2048,128]{1,0,2:T(4,128)} %reshape.46, f32[]{:T(128)} %constant.5.clone.1), dimensions={0}, to_apply=%region_0.0 | reduce | flops 786432 | bytes 5242884 | tf_op jit(solution)/shard_map/reduce_sum | solution.py:43
  88.0 0.1 fusion.6
  88.1 3.3 %multiply_convert_fusion.2 = (bf16[512,64,64]{0,2,1:T(8,128)(2,1)S(1)}, bf16[512,64,64]{0,2,1:T(8,128)(2,1)S(1)}) fusion(f32[512,64]{0,1:T(8,128)S(1)} %get-tuple-element.6, f32[512,64]{0,1:T(8,128)S(1)} %get-tuple-element.7, f32[512,64]{0,1:T(8,128)S(1)} %get-tuple-element.8, f32[512,64]{0,1:T(8,128)S(1)} %get-tuple-element.9), kind=kLoop, calls=%fused_computation.2 | loop fusion | flops 8388608 | bytes 8912896 | tf_op jit(solution)/shard_map/convert_element_type | solution.py:20
  91.4 1.3 fusion.4
  92.7 1.3 convolution_add_fusion.2
  94.0 3.3 %multiply_convert_fusion = (bf16[512,64,64]{0,2,1:T(8,128)(2,1)S(1)}, bf16[512,64,64]{0,2,1:T(8,128)(2,1)S(1)}) fusion(f32[512,64]{0,1:T(8,128)S(1)} %get-tuple-element.3, f32[512,64]{0,1:T(8,128)S(1)} %get-tuple-element.2, f32[512,64]{0,1:T(8,128)S(1)} %get-tuple-element.4, f32[512,64]{0,1:T(8,128)S(1)} %get-tuple-element.5), kind=kLoop, calls=%fused_computation | loop fusion | flops 8388608 | bytes 8912896 | tf_op jit(solution)/shard_map/convert_element_type | solution.py:20
  97.3 1.3 convolution_add_fusion.1
  98.6 1.3 fusion
  99.9 0.7 copy.11
  100.7 4.6 %all-to-all-start = ((bf16[32,8,512]{2,0,1:T(8,128)(2,1)}), bf16[32,8,512]{2,0,1:T(8,128)(2,1)S(1)}, u32[]{:S(2)}, u32[]{:S(2)}) async-start(bf16[32,8,512]{2,0,1:T(8,128)(2,1)} %bitcast.25), calls=%async_computation | async-start | bytes 524288 | tf_op jit(solution)/shard_map/all_to_all | solution.py:54
  105.9 17.8 %psum.7 = f32[]{:T(128)} all-reduce(f32[]{:T(128)S(6)} %convert_element_type.51), channel_id=1, replica_groups=mesh['dp'=8,'tensor'=4] {'dp'}, use_global_device_ids=true, to_apply=%region_2.0 | all-reduce | flops 1 | bytes 8 | tf_op jit(solution)/shard_map/psum | solution.py:50
  123.7 0.0 copy-start.1
  123.7 14.9 %all_gather.11 = bf16[256,1024]{1,0:T(8,128)(2,1)S(1)} all-gather(bf16[32,1024]{1,0:T(8,128)(2,1)S(1)} %constant_dynamic-slice_fusion), channel_id=1, replica_groups=mesh['dp'=8,'tensor'=4] {'dp'}, dimensions={0}, use_global_device_ids=true | all-gather | bytes 589824 | tf_op jit(solution)/shard_map/all_gather | solution.py:58
  138.6 0.0 all-to-all-done
  138.6 2.4 %convolution_divide_fusion = f32[512,1024]{1,0:T(8,128)} fusion(bf16[256,512]{1,0:T(8,128)(2,1)S(1)} %bitcast.32, bf16[256,1024]{1,0:T(8,128)(2,1)S(1)} %all_gather.11, f32[]{:T(128)} %psum.7), kind=kOutput, calls=%fused_computation.8 | convolution fusion | flops 268959744 | bytes 2883588 | tf_op jit(solution)/shard_map/dot_general | solution.py:29
  141.0 0.0 copy-done.1
  (2 shorter events, 0.0 us)
Async XLA Ops:
  7.2 3.7 %copy-start = (bf16[3584,64]{0,1:T(8,128)(2,1)S(1)}, bf16[3584,64]{0,1:T(8,128)(2,1)}, u32[]{:S(2)}) copy-start(bf16[3584,64]{0,1:T(8,128)(2,1)} %param.8) | copy-start | bytes 1376260
  7.2 69.9 %all-gather.3.cloned.1.call-start = ((), (), s32[]{:S(2)}) async-start(), calls=%async_computation.1 | async-start | bytes 5242880 | tf_op jit(solution)/shard_map/all_gather | solution.py:43
  10.9 11.5 %copy-start.2 = (s32[32,2048]{1,0:T(8,128)S(1)}, s32[32,2048]{1,0:T(8,128)}, u32[]{:S(2)}) copy-start(s32[32,2048]{1,0:T(8,128)} %param.10) | copy-start | bytes 786436
  100.7 38.0 %all-to-all-start = ((bf16[32,8,512]{2,0,1:T(8,128)(2,1)}), bf16[32,8,512]{2,0,1:T(8,128)(2,1)S(1)}, u32[]{:S(2)}, u32[]{:S(2)}) async-start(bf16[32,8,512]{2,0,1:T(8,128)(2,1)} %bitcast.25), calls=%async_computation | async-start | bytes 524288 | tf_op jit(solution)/shard_map/all_to_all | solution.py:54
  123.7 17.3 %copy-start.1 = (bf16[32,1024]{1,0:T(8,128)(2,1)}, bf16[32,1024]{1,0:T(8,128)(2,1)S(1)}, u32[]{:S(2)}) copy-start(bf16[32,1024]{1,0:T(8,128)(2,1)S(1)} %constant_dynamic-slice_fusion) | copy-start | bytes 196612
Sparse Core Ops, SparseCore 0:
  21.8 55.2 all-gather.2
